TPU v7x, 32 devices: a whole 2x2x4 slice. The times are simulated.
32 devices in a mesh: src: 8 (over y, x, core), tgt: 4 (over z).
Axes of the slice: x: 2, y: 2, z: 4, core: 2. Of those that a mesh axis runs over, the one named last changes fastest.
Arguments:
- src_coords: float32 [3, 49152], P(None, 'src'), may hold values from 0 to 1, as said below
- tgt_coords: float32 [3, 24576], P(None, 'tgt'), may hold values from 0 to 1
- src_scaling: float32 [32, 49152], P('tgt', 'src'), may hold values from 0.25 to 4
- src_mass: float32 [32, 49152], P('tgt', 'src'), may hold values from 0.25 to 4
- tgt_mass: float32 [32, 24576], P(None, 'tgt'), may hold values from 0.25 to 4
Outputs:
- new_src_scaling: float32 [32, 49152], P('tgt', 'src')
- tgt_scaling: float32 [32, 24576], P('src', 'tgt')
Inputs may be any that keep to these rules, and one draw needn't show every extreme that they name: `src_coords`: source points lie in the unit cube.
All inputs are finite; a program needn't handle non-finite values.
Results may differ from a plain program's by a relative error of at most 0.00036.
Values may be sent and summed in bfloat16 or wider, within the bound.
No kernel may reach another device: no remote copies, remote signals or barrier semaphores. Data moves between devices by JAX's collectives and lax.ppermute only.
A program may use at most 64 MiB of HBM per device.

v0:
```python
import jax
import jax.numpy as jnp
from jax import lax
from jax.sharding import PartitionSpec as P


def kernel_block(xb, yt):
    dist = (xb[0][:, None] - yt[0][None, :]) ** 2
    dist = dist + (xb[1][:, None] - yt[1][None, :]) ** 2
    dist = dist + (xb[2][:, None] - yt[2][None, :]) ** 2
    return (180.0 * jnp.exp(-100.0 * dist)).astype(jnp.bfloat16)


def on_device(src_coords, tgt_coords, src_scaling, src_mass, tgt_mass):
    src_pts = src_coords.shape[1]
    tgt_pts = tgt_coords.shape[1]
    weights = tgt_mass.shape[0]
    block = min(512, src_pts)
    count = src_pts // block
    xs_blocks = src_coords.reshape(3, count, block).transpose(1, 0, 2)
    src_low = lax.all_gather(src_scaling.astype(jnp.bfloat16), "tgt", axis=0, tiled=True)
    u_blocks = src_low.reshape(weights, count, block).transpose(1, 0, 2)

    def col_step(carry, items):
        xb, ub = items
        kern = kernel_block(xb, tgt_coords)
        return (carry + jnp.dot(ub, kern, preferred_element_type=jnp.float32), None)

    col_terms, _ = lax.scan(
        col_step, jnp.zeros((weights, tgt_pts), jnp.float32), (xs_blocks, u_blocks)
    )
    total_src = src_pts * lax.axis_size("src")
    share_rows = weights // lax.axis_size("src")
    col_full = lax.psum(col_terms, "src")
    scaling_full = tgt_mass / (col_full / total_src)
    tgt_scaling = lax.dynamic_slice_in_dim(
        scaling_full, lax.axis_index("src") * share_rows, share_rows, 0
    )
    tgt_low = scaling_full.astype(jnp.bfloat16)

    def row_step(xb):
        kern = kernel_block(xb, tgt_coords)
        return jnp.dot(tgt_low, kern.T, preferred_element_type=jnp.float32)

    rows = lax.map(row_step, xs_blocks)
    row_terms = rows.transpose(1, 0, 2).reshape(weights, src_pts)
    row_part = lax.psum_scatter(row_terms, "tgt", scatter_dimension=0, tiled=True)
    total_tgt = tgt_pts * lax.axis_size("tgt")
    new_src_scaling = src_mass / (row_part / total_tgt)
    return (new_src_scaling, tgt_scaling)


def solution(mesh):
    placed = (P(None, "src"), P(None, "tgt"), P("tgt", "src"), P("tgt", "src"), P(None, "tgt"))
    return jax.shard_map(
        on_device,
        mesh=mesh,
        in_specs=placed,
        out_specs=(P("tgt", "src"), P("src", "tgt")),
        check_vma=False,
    )
```

profile of v0, /device:TPU:0, one launch (start us, length us, event | category | flops | bytes accessed | tf_op | source)
XLA Modules:
  0.0 268.2 jit_solution(8683832820979956895)
XLA Ops:
  8.2 16.3 %all_gather.3 = bf16[32,6144]{1,0:T(8,128)(2,1)S(1)} all-gather(bf16[8,6144]{1,0:T(8,128)(2,1)S(1)} %convert_element_type.12), channel_id=1, replica_groups=mesh['src'=8,'tgt'=4] {'tgt'}, dimensions={0}, use_global_device_ids=true | all-gather | bytes 491520 | tf_op jit(solution)/shard_map/all_gather | solution.py:21
  25.3 76.9 %while.22 = (s32[]{:T(128)}, f32[32,6144]{1,0:T(8,128)S(1)}, bf16[12,32,512]{2,1,0:T(8,128)(2,1)S(1)}, f32[12,3,512]{2,1,0:T(4,128)}, f32[3,6144]{1,0:T(4,128)S(1)}, /*index=5*/s32[]{:T(128)}, s32[]{:T(128)}, s32[]{}, s32[]{}) while((s32[]{:T(128)}, f32[32,6144]{1,0:T(8,128)S(1)}, bf16[12,32,512]{2,1,0:T(8,128)(2,1)S(1)}, ...), condition=%wide.region_1.2_spmd.clone, body=%wide.region_0.1_spmd.clone.sunk | while | flops 236322816 | bytes 1845391 | solution.py:29
  26.2 5.5 %convolution_add_fusion.2 = f32[32,6144]{1,0:T(8,128)S(1)} fusion(f32[6144]{0:T(1024)S(1)} %bitcast.63, f32[512]{0:T(512)S(1)} %bitcast.70, f32[6144]{0:T(1024)S(1)} %bitcast.64, f32[512]{0:T(512)S(1)} %bitcast.69, f32[6144]{0:T(1024)S(1)} %bitcast.62, f32[512]{0:T(512)S(1)} %bitcast.68, f32[32,6144]{1,0:T(8,128)S(1)} %get-tuple-element.211, ...), kind=kOutput, calls=%fused_computation.10.clone.1 | convolution fusion | flops 236322816 | bytes 1685509 | tf_op jit(solution)/shard_map/while/body/eval_jaxpr/dot_general | solution.py:27
  32.6 5.5 %convolution_add_fusion.2 = f32[32,6144]{1,0:T(8,128)S(1)} fusion(f32[6144]{0:T(1024)S(1)} %bitcast.63, f32[512]{0:T(512)S(1)} %bitcast.70, f32[6144]{0:T(1024)S(1)} %bitcast.64, f32[512]{0:T(512)S(1)} %bitcast.69, f32[6144]{0:T(1024)S(1)} %bitcast.62, f32[512]{0:T(512)S(1)} %bitcast.68, f32[32,6144]{1,0:T(8,128)S(1)} %get-tuple-element.211, ...), kind=kOutput, calls=%fused_computation.10.clone.1 | convolution fusion | flops 236322816 | bytes 1685509 | tf_op jit(solution)/shard_map/while/body/eval_jaxpr/dot_general | solution.py:27
  39.0 5.5 %convolution_add_fusion.2 = f32[32,6144]{1,0:T(8,128)S(1)} fusion(f32[6144]{0:T(1024)S(1)} %bitcast.63, f32[512]{0:T(512)S(1)} %bitcast.70, f32[6144]{0:T(1024)S(1)} %bitcast.64, f32[512]{0:T(512)S(1)} %bitcast.69, f32[6144]{0:T(1024)S(1)} %bitcast.62, f32[512]{0:T(512)S(1)} %bitcast.68, f32[32,6144]{1,0:T(8,128)S(1)} %get-tuple-element.211, ...), kind=kOutput, calls=%fused_computation.10.clone.1 | convolution fusion | flops 236322816 | bytes 1685509 | tf_op jit(solution)/shard_map/while/body/eval_jaxpr/dot_general | solution.py:27
  45.4 5.5 %convolution_add_fusion.2 = f32[32,6144]{1,0:T(8,128)S(1)} fusion(f32[6144]{0:T(1024)S(1)} %bitcast.63, f32[512]{0:T(512)S(1)} %bitcast.70, f32[6144]{0:T(1024)S(1)} %bitcast.64, f32[512]{0:T(512)S(1)} %bitcast.69, f32[6144]{0:T(1024)S(1)} %bitcast.62, f32[512]{0:T(512)S(1)} %bitcast.68, f32[32,6144]{1,0:T(8,128)S(1)} %get-tuple-element.211, ...), kind=kOutput, calls=%fused_computation.10.clone.1 | convolution fusion | flops 236322816 | bytes 1685509 | tf_op jit(solution)/shard_map/while/body/eval_jaxpr/dot_general | solution.py:27
  51.8 5.5 %convolution_add_fusion.2 = f32[32,6144]{1,0:T(8,128)S(1)} fusion(f32[6144]{0:T(1024)S(1)} %bitcast.63, f32[512]{0:T(512)S(1)} %bitcast.70, f32[6144]{0:T(1024)S(1)} %bitcast.64, f32[512]{0:T(512)S(1)} %bitcast.69, f32[6144]{0:T(1024)S(1)} %bitcast.62, f32[512]{0:T(512)S(1)} %bitcast.68, f32[32,6144]{1,0:T(8,128)S(1)} %get-tuple-element.211, ...), kind=kOutput, calls=%fused_computation.10.clone.1 | convolution fusion | flops 236322816 | bytes 1685509 | tf_op jit(solution)/shard_map/while/body/eval_jaxpr/dot_general | solution.py:27
  58.3 5.5 %convolution_add_fusion.2 = f32[32,6144]{1,0:T(8,128)S(1)} fusion(f32[6144]{0:T(1024)S(1)} %bitcast.63, f32[512]{0:T(512)S(1)} %bitcast.70, f32[6144]{0:T(1024)S(1)} %bitcast.64, f32[512]{0:T(512)S(1)} %bitcast.69, f32[6144]{0:T(1024)S(1)} %bitcast.62, f32[512]{0:T(512)S(1)} %bitcast.68, f32[32,6144]{1,0:T(8,128)S(1)} %get-tuple-element.211, ...), kind=kOutput, calls=%fused_computation.10.clone.1 | convolution fusion | flops 236322816 | bytes 1685509 | tf_op jit(solution)/shard_map/while/body/eval_jaxpr/dot_general | solution.py:27
  64.7 5.5 %convolution_add_fusion.2 = f32[32,6144]{1,0:T(8,128)S(1)} fusion(f32[6144]{0:T(1024)S(1)} %bitcast.63, f32[512]{0:T(512)S(1)} %bitcast.70, f32[6144]{0:T(1024)S(1)} %bitcast.64, f32[512]{0:T(512)S(1)} %bitcast.69, f32[6144]{0:T(1024)S(1)} %bitcast.62, f32[512]{0:T(512)S(1)} %bitcast.68, f32[32,6144]{1,0:T(8,128)S(1)} %get-tuple-element.211, ...), kind=kOutput, calls=%fused_computation.10.clone.1 | convolution fusion | flops 236322816 | bytes 1685509 | tf_op jit(solution)/shard_map/while/body/eval_jaxpr/dot_general | solution.py:27
  71.1 5.5 %convolution_add_fusion.2 = f32[32,6144]{1,0:T(8,128)S(1)} fusion(f32[6144]{0:T(1024)S(1)} %bitcast.63, f32[512]{0:T(512)S(1)} %bitcast.70, f32[6144]{0:T(1024)S(1)} %bitcast.64, f32[512]{0:T(512)S(1)} %bitcast.69, f32[6144]{0:T(1024)S(1)} %bitcast.62, f32[512]{0:T(512)S(1)} %bitcast.68, f32[32,6144]{1,0:T(8,128)S(1)} %get-tuple-element.211, ...), kind=kOutput, calls=%fused_computation.10.clone.1 | convolution fusion | flops 236322816 | bytes 1685509 | tf_op jit(solution)/shard_map/while/body/eval_jaxpr/dot_general | solution.py:27
  77.5 5.5 %convolution_add_fusion.2 = f32[32,6144]{1,0:T(8,128)S(1)} fusion(f32[6144]{0:T(1024)S(1)} %bitcast.63, f32[512]{0:T(512)S(1)} %bitcast.70, f32[6144]{0:T(1024)S(1)} %bitcast.64, f32[512]{0:T(512)S(1)} %bitcast.69, f32[6144]{0:T(1024)S(1)} %bitcast.62, f32[512]{0:T(512)S(1)} %bitcast.68, f32[32,6144]{1,0:T(8,128)S(1)} %get-tuple-element.211, ...), kind=kOutput, calls=%fused_computation.10.clone.1 | convolution fusion | flops 236322816 | bytes 1685509 | tf_op jit(solution)/shard_map/while/body/eval_jaxpr/dot_general | solution.py:27
  83.9 5.5 %convolution_add_fusion.2 = f32[32,6144]{1,0:T(8,128)S(1)} fusion(f32[6144]{0:T(1024)S(1)} %bitcast.63, f32[512]{0:T(512)S(1)} %bitcast.70, f32[6144]{0:T(1024)S(1)} %bitcast.64, f32[512]{0:T(512)S(1)} %bitcast.69, f32[6144]{0:T(1024)S(1)} %bitcast.62, f32[512]{0:T(512)S(1)} %bitcast.68, f32[32,6144]{1,0:T(8,128)S(1)} %get-tuple-element.211, ...), kind=kOutput, calls=%fused_computation.10.clone.1 | convolution fusion | flops 236322816 | bytes 1685509 | tf_op jit(solution)/shard_map/while/body/eval_jaxpr/dot_general | solution.py:27
  90.3 5.5 %convolution_add_fusion.2 = f32[32,6144]{1,0:T(8,128)S(1)} fusion(f32[6144]{0:T(1024)S(1)} %bitcast.63, f32[512]{0:T(512)S(1)} %bitcast.70, f32[6144]{0:T(1024)S(1)} %bitcast.64, f32[512]{0:T(512)S(1)} %bitcast.69, f32[6144]{0:T(1024)S(1)} %bitcast.62, f32[512]{0:T(512)S(1)} %bitcast.68, f32[32,6144]{1,0:T(8,128)S(1)} %get-tuple-element.211, ...), kind=kOutput, calls=%fused_computation.10.clone.1 | convolution fusion | flops 236322816 | bytes 1685509 | tf_op jit(solution)/shard_map/while/body/eval_jaxpr/dot_general | solution.py:27
  96.7 5.5 %convolution_add_fusion.2 = f32[32,6144]{1,0:T(8,128)S(1)} fusion(f32[6144]{0:T(1024)S(1)} %bitcast.63, f32[512]{0:T(512)S(1)} %bitcast.70, f32[6144]{0:T(1024)S(1)} %bitcast.64, f32[512]{0:T(512)S(1)} %bitcast.69, f32[6144]{0:T(1024)S(1)} %bitcast.62, f32[512]{0:T(512)S(1)} %bitcast.68, f32[32,6144]{1,0:T(8,128)S(1)} %get-tuple-element.211, ...), kind=kOutput, calls=%fused_computation.10.clone.1 | convolution fusion | flops 236322816 | bytes 1685509 | tf_op jit(solution)/shard_map/while/body/eval_jaxpr/dot_general | solution.py:27
  103.4 57.3 %all-reduce.2.cloned.1.call-done = f32[32,6144]{1,0:T(8,128)} async-done(((f32[32,6144]{1,0:T(8,128)}), f32[32,6144]{1,0:T(8,128)}) %all-reduce.2.cloned.1.call-update) | async-done | bytes 786448 | tf_op jit(solution)/shard_map/psum | solution.py:34
  160.8 1.2 fusion.17
  162.0 74.1 %while.21 = (s32[]{:T(128)}, f32[12,32,512]{2,1,0:T(8,128)S(1)}, f32[12,3,512]{2,1,0:T(4,128)}, f32[3,6144]{1,0:T(4,128)S(1)}, bf16[32,6144]{1,0:T(8,128)(2,1)S(1)}, /*index=5*/s32[]{:T(128)}, s32[]{:T(128)}, s32[]{}, s32[]{}) while((s32[]{:T(128)}, f32[12,32,512]{2,1,0:T(8,128)S(1)}, f32[12,3,512]{2,1,0:T(4,128)}, f32[3,6144]{1,0:T(4,128)S(1)}, ...), condition=%wide.region_4.5_spmd, body=%wide.region_3.4_spmd.sunk | while | flops 235929600 | bytes 698501 | solution.py:45
  162.9 5.3 %fusion.28 = f32[12,32,512]{2,1,0:T(8,128)S(1)} fusion(f32[12,32,512]{2,1,0:T(8,128)S(1)} %get-tuple-element.238, s32[]{:T(128)} %get-tuple-element.237, bf16[32,6144]{1,0:T(8,128)(2,1)S(1)} %get-tuple-element.250, f32[6144]{0:T(1024)S(1)} %bitcast.66, f32[512]{0:T(512)S(1)} %bitcast.73, f32[6144]{0:T(1024)S(1)} %bitcast.67, f32[512]{0:T(512)S(1)} %bitcast.72, ...), kind=kOutput, calls=%fused_computation.3.clone.1 | convolution fusion | flops 235929600 | bytes 538628 | tf_op jit(solution)/shard_map/while/body/eval_jaxpr/dot_general | solution.py:43
  169.1 5.3 %fusion.28 = f32[12,32,512]{2,1,0:T(8,128)S(1)} fusion(f32[12,32,512]{2,1,0:T(8,128)S(1)} %get-tuple-element.238, s32[]{:T(128)} %get-tuple-element.237, bf16[32,6144]{1,0:T(8,128)(2,1)S(1)} %get-tuple-element.250, f32[6144]{0:T(1024)S(1)} %bitcast.66, f32[512]{0:T(512)S(1)} %bitcast.73, f32[6144]{0:T(1024)S(1)} %bitcast.67, f32[512]{0:T(512)S(1)} %bitcast.72, ...), kind=kOutput, calls=%fused_computation.3.clone.1 | convolution fusion | flops 235929600 | bytes 538628 | tf_op jit(solution)/shard_map/while/body/eval_jaxpr/dot_general | solution.py:43
  175.3 5.3 %fusion.28 = f32[12,32,512]{2,1,0:T(8,128)S(1)} fusion(f32[12,32,512]{2,1,0:T(8,128)S(1)} %get-tuple-element.238, s32[]{:T(128)} %get-tuple-element.237, bf16[32,6144]{1,0:T(8,128)(2,1)S(1)} %get-tuple-element.250, f32[6144]{0:T(1024)S(1)} %bitcast.66, f32[512]{0:T(512)S(1)} %bitcast.73, f32[6144]{0:T(1024)S(1)} %bitcast.67, f32[512]{0:T(512)S(1)} %bitcast.72, ...), kind=kOutput, calls=%fused_computation.3.clone.1 | convolution fusion | flops 235929600 | bytes 538628 | tf_op jit(solution)/shard_map/while/body/eval_jaxpr/dot_general | solution.py:43
  181.4 5.3 %fusion.28 = f32[12,32,512]{2,1,0:T(8,128)S(1)} fusion(f32[12,32,512]{2,1,0:T(8,128)S(1)} %get-tuple-element.238, s32[]{:T(128)} %get-tuple-element.237, bf16[32,6144]{1,0:T(8,128)(2,1)S(1)} %get-tuple-element.250, f32[6144]{0:T(1024)S(1)} %bitcast.66, f32[512]{0:T(512)S(1)} %bitcast.73, f32[6144]{0:T(1024)S(1)} %bitcast.67, f32[512]{0:T(512)S(1)} %bitcast.72, ...), kind=kOutput, calls=%fused_computation.3.clone.1 | convolution fusion | flops 235929600 | bytes 538628 | tf_op jit(solution)/shard_map/while/body/eval_jaxpr/dot_general | solution.py:43
  187.6 5.3 %fusion.28 = f32[12,32,512]{2,1,0:T(8,128)S(1)} fusion(f32[12,32,512]{2,1,0:T(8,128)S(1)} %get-tuple-element.238, s32[]{:T(128)} %get-tuple-element.237, bf16[32,6144]{1,0:T(8,128)(2,1)S(1)} %get-tuple-element.250, f32[6144]{0:T(1024)S(1)} %bitcast.66, f32[512]{0:T(512)S(1)} %bitcast.73, f32[6144]{0:T(1024)S(1)} %bitcast.67, f32[512]{0:T(512)S(1)} %bitcast.72, ...), kind=kOutput, calls=%fused_computation.3.clone.1 | convolution fusion | flops 235929600 | bytes 538628 | tf_op jit(solution)/shard_map/while/body/eval_jaxpr/dot_general | solution.py:43
  193.8 5.3 %fusion.28 = f32[12,32,512]{2,1,0:T(8,128)S(1)} fusion(f32[12,32,512]{2,1,0:T(8,128)S(1)} %get-tuple-element.238, s32[]{:T(128)} %get-tuple-element.237, bf16[32,6144]{1,0:T(8,128)(2,1)S(1)} %get-tuple-element.250, f32[6144]{0:T(1024)S(1)} %bitcast.66, f32[512]{0:T(512)S(1)} %bitcast.73, f32[6144]{0:T(1024)S(1)} %bitcast.67, f32[512]{0:T(512)S(1)} %bitcast.72, ...), kind=kOutput, calls=%fused_computation.3.clone.1 | convolution fusion | flops 235929600 | bytes 538628 | tf_op jit(solution)/shard_map/while/body/eval_jaxpr/dot_general | solution.py:43
  199.9 5.3 %fusion.28 = f32[12,32,512]{2,1,0:T(8,128)S(1)} fusion(f32[12,32,512]{2,1,0:T(8,128)S(1)} %get-tuple-element.238, s32[]{:T(128)} %get-tuple-element.237, bf16[32,6144]{1,0:T(8,128)(2,1)S(1)} %get-tuple-element.250, f32[6144]{0:T(1024)S(1)} %bitcast.66, f32[512]{0:T(512)S(1)} %bitcast.73, f32[6144]{0:T(1024)S(1)} %bitcast.67, f32[512]{0:T(512)S(1)} %bitcast.72, ...), kind=kOutput, calls=%fused_computation.3.clone.1 | convolution fusion | flops 235929600 | bytes 538628 | tf_op jit(solution)/shard_map/while/body/eval_jaxpr/dot_general | solution.py:43
  206.1 5.3 %fusion.28 = f32[12,32,512]{2,1,0:T(8,128)S(1)} fusion(f32[12,32,512]{2,1,0:T(8,128)S(1)} %get-tuple-element.238, s32[]{:T(128)} %get-tuple-element.237, bf16[32,6144]{1,0:T(8,128)(2,1)S(1)} %get-tuple-element.250, f32[6144]{0:T(1024)S(1)} %bitcast.66, f32[512]{0:T(512)S(1)} %bitcast.73, f32[6144]{0:T(1024)S(1)} %bitcast.67, f32[512]{0:T(512)S(1)} %bitcast.72, ...), kind=kOutput, calls=%fused_computation.3.clone.1 | convolution fusion | flops 235929600 | bytes 538628 | tf_op jit(solution)/shard_map/while/body/eval_jaxpr/dot_general | solution.py:43
  212.3 5.3 %fusion.28 = f32[12,32,512]{2,1,0:T(8,128)S(1)} fusion(f32[12,32,512]{2,1,0:T(8,128)S(1)} %get-tuple-element.238, s32[]{:T(128)} %get-tuple-element.237, bf16[32,6144]{1,0:T(8,128)(2,1)S(1)} %get-tuple-element.250, f32[6144]{0:T(1024)S(1)} %bitcast.66, f32[512]{0:T(512)S(1)} %bitcast.73, f32[6144]{0:T(1024)S(1)} %bitcast.67, f32[512]{0:T(512)S(1)} %bitcast.72, ...), kind=kOutput, calls=%fused_computation.3.clone.1 | convolution fusion | flops 235929600 | bytes 538628 | tf_op jit(solution)/shard_map/while/body/eval_jaxpr/dot_general | solution.py:43
  218.5 5.3 %fusion.28 = f32[12,32,512]{2,1,0:T(8,128)S(1)} fusion(f32[12,32,512]{2,1,0:T(8,128)S(1)} %get-tuple-element.238, s32[]{:T(128)} %get-tuple-element.237, bf16[32,6144]{1,0:T(8,128)(2,1)S(1)} %get-tuple-element.250, f32[6144]{0:T(1024)S(1)} %bitcast.66, f32[512]{0:T(512)S(1)} %bitcast.73, f32[6144]{0:T(1024)S(1)} %bitcast.67, f32[512]{0:T(512)S(1)} %bitcast.72, ...), kind=kOutput, calls=%fused_computation.3.clone.1 | convolution fusion | flops 235929600 | bytes 538628 | tf_op jit(solution)/shard_map/while/body/eval_jaxpr/dot_general | solution.py:43
  224.6 5.3 %fusion.28 = f32[12,32,512]{2,1,0:T(8,128)S(1)} fusion(f32[12,32,512]{2,1,0:T(8,128)S(1)} %get-tuple-element.238, s32[]{:T(128)} %get-tuple-element.237, bf16[32,6144]{1,0:T(8,128)(2,1)S(1)} %get-tuple-element.250, f32[6144]{0:T(1024)S(1)} %bitcast.66, f32[512]{0:T(512)S(1)} %bitcast.73, f32[6144]{0:T(1024)S(1)} %bitcast.67, f32[512]{0:T(512)S(1)} %bitcast.72, ...), kind=kOutput, calls=%fused_computation.3.clone.1 | convolution fusion | flops 235929600 | bytes 538628 | tf_op jit(solution)/shard_map/while/body/eval_jaxpr/dot_general | solution.py:43
  230.8 5.3 %fusion.28 = f32[12,32,512]{2,1,0:T(8,128)S(1)} fusion(f32[12,32,512]{2,1,0:T(8,128)S(1)} %get-tuple-element.238, s32[]{:T(128)} %get-tuple-element.237, bf16[32,6144]{1,0:T(8,128)(2,1)S(1)} %get-tuple-element.250, f32[6144]{0:T(1024)S(1)} %bitcast.66, f32[512]{0:T(512)S(1)} %bitcast.73, f32[6144]{0:T(1024)S(1)} %bitcast.67, f32[512]{0:T(512)S(1)} %bitcast.72, ...), kind=kOutput, calls=%fused_computation.3.clone.1 | convolution fusion | flops 235929600 | bytes 538628 | tf_op jit(solution)/shard_map/while/body/eval_jaxpr/dot_general | solution.py:43
  236.1 1.0 copy.10
  237.8 22.0 %reduce-scatter.2.cloned.1.call-done = f32[8,6144]{1,0:T(8,128)} async-done(((f32[32,6144]{1,0:T(8,128)}), f32[8,6144]{1,0:T(8,128)}) %reduce-scatter.2.cloned.1.call-update) | async-done | bytes 196624 | tf_op jit(solution)/shard_map/reduce_scatter | solution.py:47
  259.7 1.6 multiply_divide_fusion.1
  (66 shorter events, 24.7 us)
Async XLA Ops:
  7.2 153.6 %all-reduce.2.cloned.1.call-start = ((), (), s32[]{:S(2)}) async-start(), calls=%async_computation.1 | async-start | bytes 1572864 | tf_op jit(solution)/shard_map/psum | solution.py:34
  24.4 0.9 copy-start
  102.3 0.9 copy-start.1
  102.3 58.5 %copy-start.2 = (f32[32,6144]{1,0:T(8,128)S(1)}, f32[32,6144]{1,0:T(8,128)}, u32[]{:S(2)}) copy-start(f32[32,6144]{1,0:T(8,128)} %param.13) | copy-start | bytes 2359300
  103.2 156.5 %reduce-scatter.2.cloned.1.call-start = ((), (), s32[]{:S(2)}) async-start(), calls=%async_computation.2 | async-start | bytes 983040 | tf_op jit(solution)/shard_map/reduce_scatter | solution.py:47
  237.1 22.7 %copy-start.3 = (f32[8,6144]{1,0:T(8,128)S(1)}, f32[8,6144]{1,0:T(8,128)}, u32[]{:S(2)}) copy-start(f32[8,6144]{1,0:T(8,128)} %param.12) | copy-start | bytes 589828
Sparse Core Ops, SparseCore 0:
  103.3 57.4 all-reduce.1
  237.2 22.4 reduce-scatter.1
where the time goes:
time: 270 us; the launch traced here: 268 us
  matrix products  130 us (48%)
  waiting for transfers between devices  79.3 us (29%)
  local copies, waits for them, and re-layouts  24.4 us (9%)
  blocking collectives  16.3 us (6%)
  between operations  14.1 us (5%)
  other arithmetic  3.82 us (1%)
    dot_general x12, matrix products, col_step(): return (carry + jnp.dot(ub, kern, preferred_element_type=jnp.float32), None)  66.1 us
    dot_general x12, matrix products, row_step(): return jnp.dot(tgt_low, kern.T, preferred_element_type=jnp.float32)  63.5 us
    psum x1, waiting for transfers between devices, on_device(): col_full = lax.psum(col_terms, 'src')  57.3 us
    reduce_scatter x1, waiting for transfers between devices, on_device(): lax.psum_scatter(row_terms, 'tgt', scatter_dimension=0, tiled=True)  22 us
    slice x48, local copies, waits for them, and re-layouts, kernel_block(): dist = (xb[0][:, None] - yt[0][None, :]) ** 2  21 us
    all_gather x1, blocking collectives, on_device(): lax.all_gather(src_scaling.astype(jnp.bfloat16), 'tgt', axis=0, tiled=True)  16.3 us
  transfers between devices with their start and end apart: 2, of which 2 were waited for; matrix products, arithmetic and copies ran while one was open for 0% of the time, Pallas kernels for 0%

commit v1 on v0

--- a/solution.py
+++ b/solution.py
@@ -31,7 +31,7 @@
     )
     total_src = src_pts * lax.axis_size("src")
     share_rows = weights // lax.axis_size("src")
-    col_full = lax.psum(col_terms, "src")
+    col_full = jnp.sum(lax.all_gather(col_terms, "src"), axis=0)
     scaling_full = tgt_mass / (col_full / total_src)
     tgt_scaling = lax.dynamic_slice_in_dim(
         scaling_full, lax.axis_index("src") * share_rows, share_rows, 0

time: 270 us -> 288 us (1.067)
  local copies, waits for them, and re-layouts: 24.4 us -> 36.7 us
  matrix products: 130 us -> 142 us
  waiting for transfers between devices: 79.3 us -> 69.8 us
    psum x1 -> x0, waiting for transfers between devices: 57.3 us -> none  [on_device(): col_full = lax.psum(col_terms, 'src')]
    all_gather x0 -> x1, waiting for transfers between devices: none -> 47.1 us  [on_device(): col_full = jnp.sum(lax.all_gather(col_terms, 'src'), axis=0)]
    slice x48, local copies, waits for them, and re-layouts: 21 us -> 33.7 us  [kernel_block(): dist = (xb[0][:, None] - yt[0][None, :]) ** 2]
    dot_general x12, matrix products: 63.5 us -> 75.4 us  [row_step(): return jnp.dot(tgt_low, kern.T, preferred_element_type=jnp.float32)]
    reduce_sum x0 -> x1, other arithmetic: none -> 3.18 us  [on_device(): col_full = jnp.sum(lax.all_gather(col_terms, 'src'), axis=0)]
where the time goes in v1:
time: 288 us; the launch traced here: 286 us
  matrix products  142 us (49%)
  waiting for transfers between devices  69.8 us (24%)
  local copies, waits for them, and re-layouts  36.7 us (13%)
  blocking collectives  16.3 us (6%)
  between operations  14.1 us (5%)
  other arithmetic  6.61 us (2%)
    dot_general x12, matrix products, row_step(): return jnp.dot(tgt_low, kern.T, preferred_element_type=jnp.float32)  75.4 us
    dot_general x12, matrix products, col_step(): return (carry + jnp.dot(ub, kern, preferred_element_type=jnp.float32), None)  66.1 us
    all_gather x1, waiting for transfers between devices, on_device(): col_full = jnp.sum(lax.all_gather(col_terms, 'src'), axis=0)  47.1 us
    slice x48, local copies, waits for them, and re-layouts, kernel_block(): dist = (xb[0][:, None] - yt[0][None, :]) ** 2  33.7 us
    reduce_scatter x1, waiting for transfers between devices, on_device(): lax.psum_scatter(row_terms, 'tgt', scatter_dimension=0, tiled=True)  22.7 us
    all_gather x1, blocking collectives, on_device(): lax.all_gather(src_scaling.astype(jnp.bfloat16), 'tgt', axis=0, tiled=True)  16.3 us
  transfers between devices with their start and end apart: 2, of which 2 were waited for; matrix products, arithmetic and copies ran while one was open for 0% of the time, Pallas kernels for 0%

profile of v1, /device:TPU:0, one launch (start us, length us, event | category | flops | bytes accessed | tf_op | source)
XLA Modules:
  0.0 285.9 jit_solution(13032438682829651300)
XLA Ops:
  8.2 16.3 %all_gather.9 = bf16[32,6144]{1,0:T(8,128)(2,1)S(1)} all-gather(bf16[8,6144]{1,0:T(8,128)(2,1)S(1)} %convert_element_type.12), channel_id=1, replica_groups=mesh['src'=8,'tgt'=4] {'tgt'}, dimensions={0}, use_global_device_ids=true | all-gather | bytes 491520 | tf_op jit(solution)/shard_map/all_gather | solution.py:21
  24.9 89.7 %while.22 = (s32[]{:T(128)}, f32[32,6144]{1,0:T(8,128)S(1)}, bf16[12,32,512]{2,1,0:T(8,128)(2,1)S(1)}, f32[12,3,512]{2,1,0:T(4,128)}, f32[3,6144]{1,0:T(4,128)}, /*index=5*/s32[]{:T(128)}, s32[]{:T(128)}, s32[]{}, s32[]{}) while((s32[]{:T(128)}, f32[32,6144]{1,0:T(8,128)S(1)}, bf16[12,32,512]{2,1,0:T(8,128)(2,1)S(1)}, ...), condition=%wide.region_1.2_spmd.clone, body=%wide.region_0.1_spmd.clone.sunk | while | flops 236322816 | bytes 1845391 | solution.py:29
  25.8 1.1 fusion.30
  26.9 5.5 %convolution_add_fusion.2 = f32[32,6144]{1,0:T(8,128)S(1)} fusion(f32[6144]{0:T(1024)S(1)} %bitcast.65, f32[512]{0:T(512)S(1)} %bitcast.72, f32[6144]{0:T(1024)S(1)} %bitcast.66, f32[512]{0:T(512)S(1)} %bitcast.71, f32[6144]{0:T(1024)S(1)} %bitcast.64, f32[512]{0:T(512)S(1)} %bitcast.70, f32[32,6144]{1,0:T(8,128)S(1)} %get-tuple-element.211, ...), kind=kOutput, calls=%fused_computation.10.clone.1 | convolution fusion | flops 236322816 | bytes 1685509 | tf_op jit(solution)/shard_map/while/body/eval_jaxpr/dot_general | solution.py:27
  34.4 5.5 %convolution_add_fusion.2 = f32[32,6144]{1,0:T(8,128)S(1)} fusion(f32[6144]{0:T(1024)S(1)} %bitcast.65, f32[512]{0:T(512)S(1)} %bitcast.72, f32[6144]{0:T(1024)S(1)} %bitcast.66, f32[512]{0:T(512)S(1)} %bitcast.71, f32[6144]{0:T(1024)S(1)} %bitcast.64, f32[512]{0:T(512)S(1)} %bitcast.70, f32[32,6144]{1,0:T(8,128)S(1)} %get-tuple-element.211, ...), kind=kOutput, calls=%fused_computation.10.clone.1 | convolution fusion | flops 236322816 | bytes 1685509 | tf_op jit(solution)/shard_map/while/body/eval_jaxpr/dot_general | solution.py:27
  41.8 5.5 %convolution_add_fusion.2 = f32[32,6144]{1,0:T(8,128)S(1)} fusion(f32[6144]{0:T(1024)S(1)} %bitcast.65, f32[512]{0:T(512)S(1)} %bitcast.72, f32[6144]{0:T(1024)S(1)} %bitcast.66, f32[512]{0:T(512)S(1)} %bitcast.71, f32[6144]{0:T(1024)S(1)} %bitcast.64, f32[512]{0:T(512)S(1)} %bitcast.70, f32[32,6144]{1,0:T(8,128)S(1)} %get-tuple-element.211, ...), kind=kOutput, calls=%fused_computation.10.clone.1 | convolution fusion | flops 236322816 | bytes 1685509 | tf_op jit(solution)/shard_map/while/body/eval_jaxpr/dot_general | solution.py:27
  49.3 5.5 %convolution_add_fusion.2 = f32[32,6144]{1,0:T(8,128)S(1)} fusion(f32[6144]{0:T(1024)S(1)} %bitcast.65, f32[512]{0:T(512)S(1)} %bitcast.72, f32[6144]{0:T(1024)S(1)} %bitcast.66, f32[512]{0:T(512)S(1)} %bitcast.71, f32[6144]{0:T(1024)S(1)} %bitcast.64, f32[512]{0:T(512)S(1)} %bitcast.70, f32[32,6144]{1,0:T(8,128)S(1)} %get-tuple-element.211, ...), kind=kOutput, calls=%fused_computation.10.clone.1 | convolution fusion | flops 236322816 | bytes 1685509 | tf_op jit(solution)/shard_map/while/body/eval_jaxpr/dot_general | solution.py:27
  56.8 5.5 %convolution_add_fusion.2 = f32[32,6144]{1,0:T(8,128)S(1)} fusion(f32[6144]{0:T(1024)S(1)} %bitcast.65, f32[512]{0:T(512)S(1)} %bitcast.72, f32[6144]{0:T(1024)S(1)} %bitcast.66, f32[512]{0:T(512)S(1)} %bitcast.71, f32[6144]{0:T(1024)S(1)} %bitcast.64, f32[512]{0:T(512)S(1)} %bitcast.70, f32[32,6144]{1,0:T(8,128)S(1)} %get-tuple-element.211, ...), kind=kOutput, calls=%fused_computation.10.clone.1 | convolution fusion | flops 236322816 | bytes 1685509 | tf_op jit(solution)/shard_map/while/body/eval_jaxpr/dot_general | solution.py:27
  64.3 5.5 %convolution_add_fusion.2 = f32[32,6144]{1,0:T(8,128)S(1)} fusion(f32[6144]{0:T(1024)S(1)} %bitcast.65, f32[512]{0:T(512)S(1)} %bitcast.72, f32[6144]{0:T(1024)S(1)} %bitcast.66, f32[512]{0:T(512)S(1)} %bitcast.71, f32[6144]{0:T(1024)S(1)} %bitcast.64, f32[512]{0:T(512)S(1)} %bitcast.70, f32[32,6144]{1,0:T(8,128)S(1)} %get-tuple-element.211, ...), kind=kOutput, calls=%fused_computation.10.clone.1 | convolution fusion | flops 236322816 | bytes 1685509 | tf_op jit(solution)/shard_map/while/body/eval_jaxpr/dot_general | solution.py:27
  71.7 5.5 %convolution_add_fusion.2 = f32[32,6144]{1,0:T(8,128)S(1)} fusion(f32[6144]{0:T(1024)S(1)} %bitcast.65, f32[512]{0:T(512)S(1)} %bitcast.72, f32[6144]{0:T(1024)S(1)} %bitcast.66, f32[512]{0:T(512)S(1)} %bitcast.71, f32[6144]{0:T(1024)S(1)} %bitcast.64, f32[512]{0:T(512)S(1)} %bitcast.70, f32[32,6144]{1,0:T(8,128)S(1)} %get-tuple-element.211, ...), kind=kOutput, calls=%fused_computation.10.clone.1 | convolution fusion | flops 236322816 | bytes 1685509 | tf_op jit(solution)/shard_map/while/body/eval_jaxpr/dot_general | solution.py:27
  79.2 5.5 %convolution_add_fusion.2 = f32[32,6144]{1,0:T(8,128)S(1)} fusion(f32[6144]{0:T(1024)S(1)} %bitcast.65, f32[512]{0:T(512)S(1)} %bitcast.72, f32[6144]{0:T(1024)S(1)} %bitcast.66, f32[512]{0:T(512)S(1)} %bitcast.71, f32[6144]{0:T(1024)S(1)} %bitcast.64, f32[512]{0:T(512)S(1)} %bitcast.70, f32[32,6144]{1,0:T(8,128)S(1)} %get-tuple-element.211, ...), kind=kOutput, calls=%fused_computation.10.clone.1 | convolution fusion | flops 236322816 | bytes 1685509 | tf_op jit(solution)/shard_map/while/body/eval_jaxpr/dot_general | solution.py:27
  86.7 5.5 %convolution_add_fusion.2 = f32[32,6144]{1,0:T(8,128)S(1)} fusion(f32[6144]{0:T(1024)S(1)} %bitcast.65, f32[512]{0:T(512)S(1)} %bitcast.72, f32[6144]{0:T(1024)S(1)} %bitcast.66, f32[512]{0:T(512)S(1)} %bitcast.71, f32[6144]{0:T(1024)S(1)} %bitcast.64, f32[512]{0:T(512)S(1)} %bitcast.70, f32[32,6144]{1,0:T(8,128)S(1)} %get-tuple-element.211, ...), kind=kOutput, calls=%fused_computation.10.clone.1 | convolution fusion | flops 236322816 | bytes 1685509 | tf_op jit(solution)/shard_map/while/body/eval_jaxpr/dot_general | solution.py:27
  94.1 5.5 %convolution_add_fusion.2 = f32[32,6144]{1,0:T(8,128)S(1)} fusion(f32[6144]{0:T(1024)S(1)} %bitcast.65, f32[512]{0:T(512)S(1)} %bitcast.72, f32[6144]{0:T(1024)S(1)} %bitcast.66, f32[512]{0:T(512)S(1)} %bitcast.71, f32[6144]{0:T(1024)S(1)} %bitcast.64, f32[512]{0:T(512)S(1)} %bitcast.70, f32[32,6144]{1,0:T(8,128)S(1)} %get-tuple-element.211, ...), kind=kOutput, calls=%fused_computation.10.clone.1 | convolution fusion | flops 236322816 | bytes 1685509 | tf_op jit(solution)/shard_map/while/body/eval_jaxpr/dot_general | solution.py:27
  101.6 5.5 %convolution_add_fusion.2 = f32[32,6144]{1,0:T(8,128)S(1)} fusion(f32[6144]{0:T(1024)S(1)} %bitcast.65, f32[512]{0:T(512)S(1)} %bitcast.72, f32[6144]{0:T(1024)S(1)} %bitcast.66, f32[512]{0:T(512)S(1)} %bitcast.71, f32[6144]{0:T(1024)S(1)} %bitcast.64, f32[512]{0:T(512)S(1)} %bitcast.70, f32[32,6144]{1,0:T(8,128)S(1)} %get-tuple-element.211, ...), kind=kOutput, calls=%fused_computation.10.clone.1 | convolution fusion | flops 236322816 | bytes 1685509 | tf_op jit(solution)/shard_map/while/body/eval_jaxpr/dot_general | solution.py:27
  109.1 5.5 %convolution_add_fusion.2 = f32[32,6144]{1,0:T(8,128)S(1)} fusion(f32[6144]{0:T(1024)S(1)} %bitcast.65, f32[512]{0:T(512)S(1)} %bitcast.72, f32[6144]{0:T(1024)S(1)} %bitcast.66, f32[512]{0:T(512)S(1)} %bitcast.71, f32[6144]{0:T(1024)S(1)} %bitcast.64, f32[512]{0:T(512)S(1)} %bitcast.70, f32[32,6144]{1,0:T(8,128)S(1)} %get-tuple-element.211, ...), kind=kOutput, calls=%fused_computation.10.clone.1 | convolution fusion | flops 236322816 | bytes 1685509 | tf_op jit(solution)/shard_map/while/body/eval_jaxpr/dot_general | solution.py:27
  115.8 47.1 %all-gather.3.cloned.1.call-done = f32[256,6144]{1,0:T(8,128)} async-done(((f32[32,6144]{1,0:T(8,128)}), f32[256,6144]{1,0:T(8,128)}) %all-gather.3.cloned.1.call-update) | async-done | bytes 6291472 | tf_op jit(solution)/shard_map/all_gather | solution.py:34
  162.9 3.2 %reduce_sum.9 = f32[32,6144]{1,0:T(8,128)S(1)} reduce(f32[8,32,6144]{2,1,0:T(8,128)} %bitcast.60, f32[]{:T(128)} %constant.25.clone.1), dimensions={0}, to_apply=%region_2.3 | reduce | flops 1376256 | bytes 7077892 | tf_op jit(solution)/shard_map/reduce_sum | solution.py:34
  166.9 86.2 %while.21 = (s32[]{:T(128)}, f32[12,32,512]{2,1,0:T(8,128)S(1)}, f32[12,3,512]{2,1,0:T(4,128)}, f32[3,6144]{1,0:T(4,128)S(1)}, bf16[32,6144]{1,0:T(8,128)(2,1)}, /*index=5*/s32[]{:T(128)}, s32[]{:T(128)}, s32[]{}, s32[]{}) while((s32[]{:T(128)}, f32[12,32,512]{2,1,0:T(8,128)S(1)}, f32[12,3,512]{2,1,0:T(4,128)}, f32[3,6144]{1,0:T(4,128)S(1)}, ...), condition=%wide.region_4.5_spmd, body=%wide.region_3.4_spmd.sunk | while | flops 235929600 | bytes 698501 | solution.py:45
  167.8 6.3 %fusion.28 = f32[12,32,512]{2,1,0:T(8,128)S(1)} fusion(f32[12,32,512]{2,1,0:T(8,128)S(1)} %get-tuple-element.238, s32[]{:T(128)} %get-tuple-element.237, bf16[32,6144]{1,0:T(8,128)(2,1)} %get-tuple-element.250, f32[6144]{0:T(1024)S(1)} %bitcast.68, f32[512]{0:T(512)S(1)} %bitcast.75, f32[6144]{0:T(1024)S(1)} %bitcast.69, f32[512]{0:T(512)S(1)} %bitcast.74, ...), kind=kOutput, calls=%fused_computation.3.clone.1 | convolution fusion | flops 235929600 | bytes 538628 | tf_op jit(solution)/shard_map/while/body/eval_jaxpr/dot_general | solution.py:43
  175.0 6.3 %fusion.28 = f32[12,32,512]{2,1,0:T(8,128)S(1)} fusion(f32[12,32,512]{2,1,0:T(8,128)S(1)} %get-tuple-element.238, s32[]{:T(128)} %get-tuple-element.237, bf16[32,6144]{1,0:T(8,128)(2,1)} %get-tuple-element.250, f32[6144]{0:T(1024)S(1)} %bitcast.68, f32[512]{0:T(512)S(1)} %bitcast.75, f32[6144]{0:T(1024)S(1)} %bitcast.69, f32[512]{0:T(512)S(1)} %bitcast.74, ...), kind=kOutput, calls=%fused_computation.3.clone.1 | convolution fusion | flops 235929600 | bytes 538628 | tf_op jit(solution)/shard_map/while/body/eval_jaxpr/dot_general | solution.py:43
  182.1 6.3 %fusion.28 = f32[12,32,512]{2,1,0:T(8,128)S(1)} fusion(f32[12,32,512]{2,1,0:T(8,128)S(1)} %get-tuple-element.238, s32[]{:T(128)} %get-tuple-element.237, bf16[32,6144]{1,0:T(8,128)(2,1)} %get-tuple-element.250, f32[6144]{0:T(1024)S(1)} %bitcast.68, f32[512]{0:T(512)S(1)} %bitcast.75, f32[6144]{0:T(1024)S(1)} %bitcast.69, f32[512]{0:T(512)S(1)} %bitcast.74, ...), kind=kOutput, calls=%fused_computation.3.clone.1 | convolution fusion | flops 235929600 | bytes 538628 | tf_op jit(solution)/shard_map/while/body/eval_jaxpr/dot_general | solution.py:43
  189.3 6.3 %fusion.28 = f32[12,32,512]{2,1,0:T(8,128)S(1)} fusion(f32[12,32,512]{2,1,0:T(8,128)S(1)} %get-tuple-element.238, s32[]{:T(128)} %get-tuple-element.237, bf16[32,6144]{1,0:T(8,128)(2,1)} %get-tuple-element.250, f32[6144]{0:T(1024)S(1)} %bitcast.68, f32[512]{0:T(512)S(1)} %bitcast.75, f32[6144]{0:T(1024)S(1)} %bitcast.69, f32[512]{0:T(512)S(1)} %bitcast.74, ...), kind=kOutput, calls=%fused_computation.3.clone.1 | convolution fusion | flops 235929600 | bytes 538628 | tf_op jit(solution)/shard_map/while/body/eval_jaxpr/dot_general | solution.py:43
  196.5 6.3 %fusion.28 = f32[12,32,512]{2,1,0:T(8,128)S(1)} fusion(f32[12,32,512]{2,1,0:T(8,128)S(1)} %get-tuple-element.238, s32[]{:T(128)} %get-tuple-element.237, bf16[32,6144]{1,0:T(8,128)(2,1)} %get-tuple-element.250, f32[6144]{0:T(1024)S(1)} %bitcast.68, f32[512]{0:T(512)S(1)} %bitcast.75, f32[6144]{0:T(1024)S(1)} %bitcast.69, f32[512]{0:T(512)S(1)} %bitcast.74, ...), kind=kOutput, calls=%fused_computation.3.clone.1 | convolution fusion | flops 235929600 | bytes 538628 | tf_op jit(solution)/shard_map/while/body/eval_jaxpr/dot_general | solution.py:43
  203.7 6.3 %fusion.28 = f32[12,32,512]{2,1,0:T(8,128)S(1)} fusion(f32[12,32,512]{2,1,0:T(8,128)S(1)} %get-tuple-element.238, s32[]{:T(128)} %get-tuple-element.237, bf16[32,6144]{1,0:T(8,128)(2,1)} %get-tuple-element.250, f32[6144]{0:T(1024)S(1)} %bitcast.68, f32[512]{0:T(512)S(1)} %bitcast.75, f32[6144]{0:T(1024)S(1)} %bitcast.69, f32[512]{0:T(512)S(1)} %bitcast.74, ...), kind=kOutput, calls=%fused_computation.3.clone.1 | convolution fusion | flops 235929600 | bytes 538628 | tf_op jit(solution)/shard_map/while/body/eval_jaxpr/dot_general | solution.py:43
  210.9 6.3 %fusion.28 = f32[12,32,512]{2,1,0:T(8,128)S(1)} fusion(f32[12,32,512]{2,1,0:T(8,128)S(1)} %get-tuple-element.238, s32[]{:T(128)} %get-tuple-element.237, bf16[32,6144]{1,0:T(8,128)(2,1)} %get-tuple-element.250, f32[6144]{0:T(1024)S(1)} %bitcast.68, f32[512]{0:T(512)S(1)} %bitcast.75, f32[6144]{0:T(1024)S(1)} %bitcast.69, f32[512]{0:T(512)S(1)} %bitcast.74, ...), kind=kOutput, calls=%fused_computation.3.clone.1 | convolution fusion | flops 235929600 | bytes 538628 | tf_op jit(solution)/shard_map/while/body/eval_jaxpr/dot_general | solution.py:43
  218.1 6.3 %fusion.28 = f32[12,32,512]{2,1,0:T(8,128)S(1)} fusion(f32[12,32,512]{2,1,0:T(8,128)S(1)} %get-tuple-element.238, s32[]{:T(128)} %get-tuple-element.237, bf16[32,6144]{1,0:T(8,128)(2,1)} %get-tuple-element.250, f32[6144]{0:T(1024)S(1)} %bitcast.68, f32[512]{0:T(512)S(1)} %bitcast.75, f32[6144]{0:T(1024)S(1)} %bitcast.69, f32[512]{0:T(512)S(1)} %bitcast.74, ...), kind=kOutput, calls=%fused_computation.3.clone.1 | convolution fusion | flops 235929600 | bytes 538628 | tf_op jit(solution)/shard_map/while/body/eval_jaxpr/dot_general | solution.py:43
  225.3 6.3 %fusion.28 = f32[12,32,512]{2,1,0:T(8,128)S(1)} fusion(f32[12,32,512]{2,1,0:T(8,128)S(1)} %get-tuple-element.238, s32[]{:T(128)} %get-tuple-element.237, bf16[32,6144]{1,0:T(8,128)(2,1)} %get-tuple-element.250, f32[6144]{0:T(1024)S(1)} %bitcast.68, f32[512]{0:T(512)S(1)} %bitcast.75, f32[6144]{0:T(1024)S(1)} %bitcast.69, f32[512]{0:T(512)S(1)} %bitcast.74, ...), kind=kOutput, calls=%fused_computation.3.clone.1 | convolution fusion | flops 235929600 | bytes 538628 | tf_op jit(solution)/shard_map/while/body/eval_jaxpr/dot_general | solution.py:43
  232.4 6.3 %fusion.28 = f32[12,32,512]{2,1,0:T(8,128)S(1)} fusion(f32[12,32,512]{2,1,0:T(8,128)S(1)} %get-tuple-element.238, s32[]{:T(128)} %get-tuple-element.237, bf16[32,6144]{1,0:T(8,128)(2,1)} %get-tuple-element.250, f32[6144]{0:T(1024)S(1)} %bitcast.68, f32[512]{0:T(512)S(1)} %bitcast.75, f32[6144]{0:T(1024)S(1)} %bitcast.69, f32[512]{0:T(512)S(1)} %bitcast.74, ...), kind=kOutput, calls=%fused_computation.3.clone.1 | convolution fusion | flops 235929600 | bytes 538628 | tf_op jit(solution)/shard_map/while/body/eval_jaxpr/dot_general | solution.py:43
  239.6 6.3 %fusion.28 = f32[12,32,512]{2,1,0:T(8,128)S(1)} fusion(f32[12,32,512]{2,1,0:T(8,128)S(1)} %get-tuple-element.238, s32[]{:T(128)} %get-tuple-element.237, bf16[32,6144]{1,0:T(8,128)(2,1)} %get-tuple-element.250, f32[6144]{0:T(1024)S(1)} %bitcast.68, f32[512]{0:T(512)S(1)} %bitcast.75, f32[6144]{0:T(1024)S(1)} %bitcast.69, f32[512]{0:T(512)S(1)} %bitcast.74, ...), kind=kOutput, calls=%fused_computation.3.clone.1 | convolution fusion | flops 235929600 | bytes 538628 | tf_op jit(solution)/shard_map/while/body/eval_jaxpr/dot_general | solution.py:43
  246.8 6.3 %fusion.28 = f32[12,32,512]{2,1,0:T(8,128)S(1)} fusion(f32[12,32,512]{2,1,0:T(8,128)S(1)} %get-tuple-element.238, s32[]{:T(128)} %get-tuple-element.237, bf16[32,6144]{1,0:T(8,128)(2,1)} %get-tuple-element.250, f32[6144]{0:T(1024)S(1)} %bitcast.68, f32[512]{0:T(512)S(1)} %bitcast.75, f32[6144]{0:T(1024)S(1)} %bitcast.69, f32[512]{0:T(512)S(1)} %bitcast.74, ...), kind=kOutput, calls=%fused_computation.3.clone.1 | convolution fusion | flops 235929600 | bytes 538628 | tf_op jit(solution)/shard_map/while/body/eval_jaxpr/dot_general | solution.py:43
  254.8 22.7 %reduce-scatter.2.cloned.1.call-done = f32[8,6144]{1,0:T(8,128)} async-done(((f32[32,6144]{1,0:T(8,128)}), f32[8,6144]{1,0:T(8,128)}) %reduce-scatter.2.cloned.1.call-update) | async-done | bytes 196624 | tf_op jit(solution)/shard_map/reduce_scatter | solution.py:47
  277.4 1.6 multiply_divide_fusion.1
  (67 shorter events, 37.7 us)
Async XLA Ops:
  7.2 155.7 %all-gather.3.cloned.1.call-start = ((), (), s32[]{:S(2)}) async-start(), calls=%async_computation.2 | async-start | bytes 7077888 | tf_op jit(solution)/shard_map/all_gather | solution.py:34
  114.6 0.9 copy-start.1
  114.6 51.4 %copy-start.2 = (f32[32,6144]{1,0:T(8,128)S(1)}, f32[32,6144]{1,0:T(8,128)}, u32[]{:S(2)}) copy-start(f32[32,6144]{1,0:T(8,128)} %param.13) | copy-start | bytes 2359300
  114.6 52.3 %copy-start = (f32[3,6144]{1,0:T(4,128)S(1)}, f32[3,6144]{1,0:T(4,128)}, u32[]{:S(2)}) copy-start(f32[3,6144]{1,0:T(4,128)} %get-tuple-element.258) | copy-start | bytes 221188
  115.6 161.9 %reduce-scatter.2.cloned.1.call-start = ((), (), s32[]{:S(2)}) async-start(), calls=%async_computation.1 | async-start | bytes 983040 | tf_op jit(solution)/shard_map/reduce_scatter | solution.py:47
  166.9 110.5 %copy-start.3 = (f32[8,6144]{1,0:T(8,128)S(1)}, f32[8,6144]{1,0:T(8,128)}, u32[]{:S(2)}) copy-start(f32[8,6144]{1,0:T(8,128)} %param.12) | copy-start | bytes 589828
Sparse Core Ops, SparseCore 0:
  115.7 47.1 all-gather.2
  254.2 23.1 reduce-scatter.1
